TPU v7x, 32 devices: a whole 2x2x4 slice. The times are simulated.
32 devices in a mesh: dp: 16 (over z, x, core), seq: 2 (over y).
Axes of the slice: x: 2, y: 2, z: 4, core: 2. Of those that a mesh axis runs over, the one named last changes fastest.
Arguments:
- video: bfloat16 [16, 256, 3072], P('dp', 'seq'), may hold values from -6 to 6
- shift: float32 [16, 3072], P('dp'), may hold values from -5 to 5
- scale: float32 [16, 3072], P('dp'), may hold values from -2.5 to 2.5
- project_weight: bfloat16 [3, 3072, 2048], P(None, 'dp', 'seq'), may hold values from -0.109375 to 0.109375
- project_bias: float32 [3, 2048], P(None, 'seq'), may hold values from -3 to 3
- query_gain: float32 [128], replicated, may hold values from 0.5 to 12
- key_gain: float32 [128], replicated, may hold values from 0.5 to 12
- tile_table: int32 [16, 16, 12], P('dp'), may hold values from 0 to 15, as said below
Outputs:
- attended: bfloat16 [16, 256, 2048], P('dp', 'seq')
Inputs may be any that keep to these rules, and one draw needn't show every extreme that they name: `tile_table`: for query tile t of frame f = t // 8, row (t % 8) // 4 and column t % 4 of the 2 x 4 grid of tiles of a frame, the entries are the tiles of 2 consecutive frames, both rows and 3 consecutive columns that contain t, listed with the frame changing slowest and the column fastest (slot s: frame step s // 6, row s % 6 // 3, column step s % 3); the window's placement varies from tile to tile.
All inputs are finite; a program needn't handle non-finite values.
Results may differ from a plain program's by a relative error of at most 0.005.
The roundings to bfloat16 on the way count: a program that leaves them out, or rounds other values in their place, can miss the bound.
Values may be sent and summed in bfloat16 or wider, within the bound.
A program may use at most 128 MiB of HBM per device.

v0:
```python
import jax
import jax.numpy as jnp
from jax import lax
from jax.experimental import pallas as pl
from jax.experimental.pallas import tpu as pltpu
from jax.sharding import PartitionSpec as P

HD = 128
TILE = 16
LANES = 128


EPS = 1e-06
MASKED = -1e30
CHUNKS = 2
MESH = pl.DeviceIdType.MESH


def rms_norm(values_in, gain):
    return (
        values_in * lax.rsqrt(jnp.mean(values_in * values_in, axis=-1, keepdims=True) + EPS) * gain
    ).astype(jnp.bfloat16)


def window_attention(projected, query_gain, key_gain, table):
    seqlen = projected.shape[1]
    heads = projected.shape[2] // HD
    ntiles = seqlen // TILE
    ktiles = table.shape[1]
    queries = rms_norm(projected[0].reshape(seqlen, heads, HD), query_gain)
    keys = rms_norm(projected[1].reshape(seqlen, heads, HD), key_gain)
    values = projected[2].reshape(seqlen, heads, HD).astype(jnp.bfloat16)
    query_tiles = queries.reshape(ntiles, TILE, heads, HD)
    key_sel = jnp.take(keys.reshape(ntiles, TILE, heads, HD), table, axis=0).reshape(
        ntiles, ktiles * TILE, heads, HD
    )
    value_sel = jnp.take(values.reshape(ntiles, TILE, heads, HD), table, axis=0).reshape(
        ntiles, ktiles * TILE, heads, HD
    )
    scores = jnp.einsum(
        "nqhd,nkhd->nhqk", query_tiles, key_sel, preferred_element_type=jnp.float32
    ) * HD ** (-0.5)
    largest = jnp.max(scores, axis=-1, keepdims=True)
    expo = jnp.exp(scores - largest)
    weights = (expo / jnp.sum(expo, axis=-1, keepdims=True)).astype(jnp.bfloat16)
    result = jnp.einsum("nhqk,nkhd->nqhd", weights, value_sel, preferred_element_type=jnp.float32)
    return result.astype(jnp.bfloat16).reshape(seqlen, heads * HD)


def gathered_device(video, shift, scale, project_weight, project_bias, query_gain, key_gain, tile_table):
    tokens = video[0].astype(jnp.float32)
    centre = jnp.mean(tokens, axis=-1, keepdims=True)
    spread = jnp.mean((tokens - centre) ** 2, axis=-1, keepdims=True)
    normed = ((tokens - centre) * lax.rsqrt(spread + EPS) * (1.0 + scale[0]) + shift[0]).astype(
        jnp.bfloat16
    )
    gathered = lax.all_gather(normed, "seq", axis=0, tiled=True)
    projected = jnp.einsum(
        "sd,tdc->tsc",
        gathered,
        lax.all_gather(project_weight, "dp", axis=1, tiled=True),
        preferred_element_type=jnp.float32,
    )
    projected = projected + project_bias[:, None, :]
    local_heads = window_attention(projected, query_gain, key_gain, tile_table[0])
    returned = lax.all_to_all(local_heads, "seq", split_axis=0, concat_axis=1, tiled=True)
    return returned[None]


def layer_kernel(
    video_hbm,
    shift_hbm,
    scale_hbm,
    member_ref,
    bias_hbm,
    qgain_hbm,
    kgain_hbm,
    weight_ref,
    out_ref,
    video_ref,
    shift_ref,
    scale_ref,
    bias_ref,
    qgain_ref,
    kgain_ref,
    wbuf,
    tok,
    obuf,
    own_sem,
    small_sem,
    wsend,
    zsend,
    wrecv,
    tsend,
    trecv,
    osend,
    orecv,
):
    dp = lax.axis_index("dp")
    y = lax.axis_index("seq")
    core = lax.rem(dp, 2)
    x = lax.rem(dp // 2, 2)
    z = dp // 4
    rows, width = video_ref.shape
    slab = weight_ref.shape[1]
    end = jnp.logical_or(z == 0, z == 3)
    inner = jnp.logical_not(end)
    mate = 1 + z // 3
    far = 3 * (z // 2)
    peer = 3 - z

    def pos(k):
        xk = 1 - x if k & 2 else x
        ck = 1 - core if k & 1 else core
        return xk * 2 + ck

    def at(k, flip=0, layer=None):
        return ((z if layer is None else layer) * 4 + pos(k), 1 - y if flip else y)

    small = [
        pltpu.make_async_copy(src, dst, small_sem.at[n])
        for n, (src, dst) in enumerate(
            [
                (video_hbm, video_ref),
                (shift_hbm, shift_ref),
                (scale_hbm, scale_ref),
                (bias_hbm, bias_ref),
                (qgain_hbm, qgain_ref),
                (kgain_hbm, kgain_ref),
            ]
        )
    ]

    barrier = pltpu.get_barrier_semaphore()

    def greet(target):
        pl.semaphore_signal(barrier, inc=1, device_id=target, device_id_type=MESH)

    for flip in range(2):
        for k in range(4):
            if k or flip:
                greet(at(k, flip))

    @pl.when(end)
    def _():
        for flip in range(2):
            for k in range(4):
                greet(at(k, flip, mate))

    @pl.when(inner)
    def _():
        for flip in range(2):
            for k in range(4):
                greet(at(k, flip, far))
        greet(at(0, 0, peer))

    def block(h, owner):
        return wbuf.at[h, pl.ds(pl.multiple_of(owner * slab, 16), slab), :]

    def columns(place, h):
        return pl.ds(pl.multiple_of((place * 2 + h) * HD, HD), HD)

    mine = pl.ds(pl.multiple_of(dp * slab, 16), slab)

    for h in range(2):
        for i in range(3):
            pltpu.make_async_copy(
                weight_ref.at[i, :, columns(pos(0), h)],
                wbuf.at[h, mine, pl.ds(i * HD, HD)],
                own_sem.at[h],
            ).start()
        if h == 0:
            for copy in small:
                copy.start()

    @pl.when(end)
    def _():
        pl.semaphore_wait(barrier, 15)

    @pl.when(inner)
    def _():
        pl.semaphore_wait(barrier, 16)

    def remote(src, dst, send, recv, target):
        return pltpu.make_async_remote_copy(
            src_ref=src,
            dst_ref=dst,
            send_sem=send,
            recv_sem=recv,
            device_id=target,
            device_id_type=MESH,
        )

    def piece_sends(h, k):
        return [
            remote(
                weight_ref.at[i, :, columns(pos(k), h)],
                wbuf.at[h, mine, pl.ds(i * HD, HD)],
                wsend.at[h, k - 1, i],
                wrecv.at[h, dp],
                at(k),
            )
            for i in range(3)
        ]

    def z_send(h, owner, way, layer):
        return remote(
            block(h, owner),
            block(h, owner),
            zsend.at[h, owner, way],
            wrecv.at[h, owner],
            at(0, 0, layer),
        )

    def wait_block(h, owner):
        remote(
            block(h, owner), block(h, owner), zsend.at[h, owner, 0], wrecv.at[h, owner], at(1)
        ).wait_recv()

    def wait_own(h, k):
        owner = z * 4 + pos(k)
        if k:
            wait_block(h, owner)
        else:
            pltpu.make_async_copy(block(h, owner), block(h, owner), own_sem.at[h]).wait()

    def ways(h, layer, role):
        if role == "end":
            return [(0, mate)] if layer is z else []
        if layer is peer or layer is far_peer:
            return [(0, far)] if h == 0 else []
        if layer is far:
            return [(1, peer)]
        return [(1, peer), (0, far)] if h == 0 else [(1, peer)]

    far_peer = 3 - far

    def pass_on(h, layer, k, role):
        for way, target in ways(h, layer, role):
            z_send(h, layer * 4 + pos(k), way, target).start()

    def own_layer(h, ks, role):
        for k in ks:
            wait_own(h, k)
            pass_on(h, z, k, role)

    def relay(h, layers, role):
        for k in range(4):
            for layer in layers:
                wait_block(h, layer * 4 + pos(k))
                pass_on(h, layer, k, role)

    for k in (2, 3, 1):
        for copy in piece_sends(0, k):
            copy.start()

    @pl.when(end)
    def _():
        own_layer(0, (0, 1), "end")

    @pl.when(inner)
    def _():
        own_layer(0, (0, 1), "inner")

    for copy in small:
        copy.wait()
    step = 16
    part = rows // CHUNKS

    def norm_chunk(q):
        half = pl.multiple_of(y * rows + q * part, TILE)

        @pl.loop(0, part // step)
        def _(n):
            first = pl.multiple_of(n * step, step)
            tokens = video_ref[pl.ds(q * part + first, step), :].astype(jnp.float32)
            centre = jnp.mean(tokens, axis=-1, keepdims=True)
            shifted = tokens - centre
            spread = jnp.mean(shifted * shifted, axis=-1, keepdims=True)
            normed = shifted * lax.rsqrt(spread + EPS) * (1.0 + scale_ref[...]) + shift_ref[...]
            tok[0, pos(0), pl.ds(half + first, step), 0:width] = normed.astype(jnp.bfloat16)

        tok[0, pos(0), pl.ds(half, part), width : width + LANES] = member_ref[
            q * part : (q + 1) * part, :
        ]

    def tokens_at(group, place, side, q):
        first = pl.multiple_of(side * rows + q * part, TILE)
        return tok.at[group, place, pl.ds(first, part), :]

    def token_send(n, group, place, side, q, target, to_group=None):
        to_group = group if to_group is None else to_group
        return remote(
            tokens_at(group, place, side, q),
            tokens_at(to_group, place, side, q),
            tsend.at[to_group, n, q],
            trecv.at[to_group, place, side, q],
            target,
        )

    def wait_tokens(group, place, side, q):
        token_send(0, group, place, side, q, at(1)).wait_recv()

    own, beside, across, diagonal = (
        (pos(0), y),
        (pos(2), y),
        (pos(0), 1 - y),
        (pos(2), 1 - y),
    )

    def own_tokens(q):
        return [
            token_send(0, 0, *own, q, at(2)),
            token_send(1, 0, *own, q, at(0, 1)),
            token_send(2, 0, *own, q, at(1)),
        ]

    def passed_tokens(q):
        return [
            token_send(3, 0, *beside, q, at(0, 1)),
            token_send(4, 0, *beside, q, at(1)),
            token_send(5, 0, *across, q, at(1)),
            token_send(6, 0, *diagonal, q, at(1)),
        ]

    def end_tokens(q):
        return [
            token_send(6, 0, *own, q, at(0, 0, mate), 1),
            token_send(7, 0, *diagonal, q, at(0, 0, mate), 1),
        ]

    def shared_tokens(q):
        return [
            token_send(0, 1, *own, q, at(2)),
            token_send(1, 1, *own, q, at(0, 1)),
            token_send(2, 1, *own, q, at(1)),
            token_send(3, 1, *beside, q, at(1)),
            token_send(4, 1, *across, q, at(1)),
            token_send(5, 1, *diagonal, q, at(1)),
        ]

    def wait_sibling_tokens(group):
        for place in (pos(1), pos(3)):
            for side in (y, 1 - y):
                for q in range(CHUNKS):
                    wait_tokens(group, place, side, q)

    total = 2 * rows
    spread_tiles = (
        lax.broadcasted_iota(jnp.int32, (LANES, total), 1) // TILE
        == lax.broadcasted_iota(jnp.int32, (LANES, total), 0)
    ).astype(jnp.bfloat16)

    def out_copy(group, h, v, side):
        return remote(
            obuf.at[group + h, v, pl.ds(side * rows, rows), :],
            out_ref.at[:, columns(y * 4 + pos(0), h)],
            osend.at[group + h, v, side],
            orecv.at[h, y, pos(0)],
            ((far if group else z) * 4 + v, side),
        )

    def attend(group, h, v):
        normed = tok[group, v, :, 0:width]
        acc = jnp.dot(normed, wbuf[h], preferred_element_type=jnp.float32)
        place = columns(pos(0), h)
        query = acc[:, 0:HD] + bias_ref[0:1, place]
        key = acc[:, HD : 2 * HD] + bias_ref[1:2, place]
        value = acc[:, 2 * HD : 3 * HD] + bias_ref[2:3, place]
        queries = rms_norm(query, qgain_ref[...])
        keys = rms_norm(key, kgain_ref[...])
        scores = lax.dot_general(
            queries, keys, (((1,), (1,)), ((), ())), preferred_element_type=jnp.float32
        ) * HD ** (-0.5)
        seen = jnp.dot(
            tok[group, v, :, width : width + LANES],
            spread_tiles,
            preferred_element_type=jnp.float32,
        )
        scores = jnp.where(seen > 0.5, scores, MASKED)
        largest = jnp.max(scores, axis=-1, keepdims=True)
        expo = jnp.exp(scores - largest)
        weights = (expo / jnp.sum(expo, axis=-1, keepdims=True)).astype(jnp.bfloat16)
        result = jnp.dot(
            weights, value.astype(jnp.bfloat16), preferred_element_type=jnp.float32
        ).astype(jnp.bfloat16)
        obuf[group + h, v] = result
        for side in range(2):
            if group:
                out_copy(group, h, v, side).start()
                continue
            away = jnp.logical_or(v != pos(0), side != y)

            @pl.when(away)
            def _():
                out_copy(group, h, v, side).start()

            @pl.when(jnp.logical_not(away))
            def _():
                out_ref[:, columns(y * 4 + pos(0), h)] = result[side * rows : (side + 1) * rows, :]

    def attend_all(group, h):
        @pl.loop(0, 4)
        def _(v):
            attend(group, h, v)

    def outs_sent(group, h):
        for v in range(4):
            for side in range(2):
                if group:
                    out_copy(group, h, v, side).wait_send()
                    continue

                @pl.when(jnp.logical_or(v != pos(0), side != y))
                def _():
                    out_copy(group, h, v, side).wait_send()

    def outs_received(h, whole):
        for flip in range(2):
            for k in range(4):
                if k or flip or whole:
                    side = 1 - y if flip else y
                    remote(
                        obuf.at[h, 0, pl.ds(0, rows), :],
                        out_ref.at[:, columns(side * 4 + pos(k), h)],
                        osend.at[h, 0, 0],
                        orecv.at[h, side, pos(k)],
                        at(1),
                    ).wait_recv()

    def z_sent(h, layer, role):
        for k in range(4):
            for way, target in ways(h, layer, role):
                z_send(h, layer * 4 + pos(k), way, target).wait_send()

    def start(copies):
        for copy in copies:
            copy.start()

    def sent(copies):
        for copy in copies:
            copy.wait_send()

    chunks = range(CHUNKS)

    def norm_and_send(first, last):
        for q in range(first, last):
            norm_chunk(q)
            start(own_tokens(q))

    def pass_direct():
        for q in chunks:
            copies = passed_tokens(q)
            wait_tokens(0, *across, q)
            copies[2].start()
            wait_tokens(0, *beside, q)
            copies[0].start()
            copies[1].start()

    norm_and_send(0, CHUNKS // 2)

    @pl.when(end)
    def _():
        own_layer(0, (2, 3), "end")
        for q in range(CHUNKS // 2):
            end_tokens(q)[0].start()

    @pl.when(inner)
    def _():
        own_layer(0, (2, 3), "inner")

    norm_and_send(CHUNKS // 2, CHUNKS)
    for k in (2, 3, 1):
        start(piece_sends(1, k))

    @pl.when(end)
    def _():
        for q in range(CHUNKS // 2, CHUNKS):
            end_tokens(q)[0].start()
        pass_direct()
        own_layer(1, range(4), "end")
        for q in chunks:
            wait_tokens(0, *diagonal, q)
            end_tokens(q)[1].start()
            passed_tokens(q)[3].start()
        relay(0, [mate], "end")
        relay(0, [3 - mate], "end")
        relay(0, [3 - z], "end")
        wait_sibling_tokens(0)
        attend_all(0, 0)
        outs_received(0, False)
        outs_received(1, True)
        outs_sent(0, 0)
        for q in chunks:
            sent(own_tokens(q) + passed_tokens(q) + end_tokens(q))
        for h in range(2):
            z_sent(h, z, "end")

    @pl.when(inner)
    def _():
        relay(0, [far, peer], "inner")
        own_layer(1, (0, 1), "inner")
        pass_direct()
        relay(0, [far_peer], "inner")
        for q in chunks:
            wait_tokens(1, *own, q)
            start(shared_tokens(q)[:3])
        own_layer(1, (2, 3), "inner")
        for q in chunks:
            wait_tokens(0, *diagonal, q)
            passed_tokens(q)[3].start()
        relay(1, [far], "inner")
        wait_sibling_tokens(0)
        attend_all(0, 0)
        for q in chunks:
            wait_tokens(1, *beside, q)
            shared_tokens(q)[3].start()
        relay(1, [peer, far_peer], "inner")
        attend_all(0, 1)
        for q in chunks:
            copies = shared_tokens(q)
            wait_tokens(1, *across, q)
            copies[4].start()
            wait_tokens(1, *diagonal, q)
            copies[5].start()
        wait_sibling_tokens(1)
        attend_all(1, 1)
        for h in range(2):
            outs_received(h, False)
            outs_sent(0, h)
        outs_sent(1, 1)
        for q in chunks:
            sent(own_tokens(q) + passed_tokens(q) + shared_tokens(q))
        for layer in (z, far, peer, far_peer):
            for h in range(2):
                z_sent(h, layer, "inner")

    for h in range(2):
        for k in (1, 2, 3):
            sent(piece_sends(h, k))


def layer_device(video, shift, scale, project_weight, project_bias, query_gain, key_gain, tile_table):
    rows, width = video.shape[1:]
    slab, columns = project_weight.shape[1:]
    tiles = rows // TILE
    table = lax.dynamic_slice_in_dim(tile_table[0], lax.axis_index("seq") * tiles, tiles, 0)
    member = jnp.any(table[:, :, None] == jnp.arange(LANES, dtype=jnp.int32), axis=1)
    member = jnp.repeat(member.astype(jnp.bfloat16), TILE, axis=0)
    vmem = pl.BlockSpec(memory_space=pltpu.VMEM)
    anywhere = pl.BlockSpec(memory_space=pl.ANY)
    dma = pltpu.SemaphoreType.DMA
    small = (video[0], shift, scale, project_bias, query_gain[None], key_gain[None])
    out = pl.pallas_call(
        layer_kernel,
        out_shape=jax.ShapeDtypeStruct((rows, 2 * columns), jnp.bfloat16),
        in_specs=[anywhere] * 3 + [vmem] + [anywhere] * 4,
        out_specs=vmem,
        scratch_shapes=[pltpu.VMEM(array.shape, array.dtype) for array in small]
        + [
            pltpu.VMEM((2, 16 * slab, 3 * HD), jnp.bfloat16),
            pltpu.VMEM((2, 4, 2 * rows, width + LANES), jnp.bfloat16),
            pltpu.VMEM((3, 4, 2 * rows, HD), jnp.bfloat16),
            dma((2,)),
            dma((6,)),
            dma((2, 3, 3)),
            dma((2, 16, 2)),
            dma((2, 16)),
            dma((2, 8, CHUNKS)),
            dma((2, 4, 2, CHUNKS)),
            dma((3, 4, 2)),
            dma((2, 2, 4)),
        ],
        compiler_params=pltpu.CompilerParams(
            collective_id=0, has_side_effects=True, vmem_limit_bytes=60 << 20
        ),
    )(*small[:3], member, *small[3:], project_weight)
    return out[None]


def solution(mesh):
    def per_device(*operands):
        video, project_weight = operands[0], operands[3]
        fits = (
            mesh.shape["dp"] == 16
            and mesh.shape["seq"] == 2
            and video.shape[0] == 1
            and project_weight.shape[2] == 8 * HD
            and video.shape[1] % (CHUNKS * TILE) == 0
            and 2 * video.shape[1] // TILE <= LANES
            and video.shape[1] <= 256
        )
        if fits:
            return layer_device(*operands)
        return gathered_device(*operands)

    return jax.shard_map(
        per_device,
        mesh=mesh,
        in_specs=(
            P("dp", "seq", None),
            P("dp", None),
            P("dp", None),
            P(None, "dp", "seq"),
            P(None, "seq"),
            P(),
            P(),
            P("dp", None, None),
        ),
        out_specs=P("dp", "seq", None),
        check_vma=False,
    )
```

profile of v0, /device:TPU:3, one launch (start us, length us, event | category | flops | bytes accessed | tf_op | source)
XLA Modules:
  0.0 84.4 jit_solution(4638987341772544231)
XLA Ops:
  0.0 0.0 copy-start
  0.0 0.7 copy-done
  0.7 0.1 constant_dynamic-slice_fusion
  0.8 0.1 fusion
  0.9 0.6 broadcast_in_dim.14
  1.5 81.0 %shard_map.82 = bf16[128,2048]{1,0:T(8,128)(2,1)} custom-call(bf16[128,3072]{1,0:T(8,128)(2,1)} %bitcast.10, f32[1,3072]{1,0:T(1,128)} %shift_hbm.1, f32[1,3072]{1,0:T(1,128)} %scale_hbm.1, bf16[128,128]{1,0:T(8,128)(2,1)} %bitcast.11, f32[3,1024]{1,0:T(4,128)} %bias_hbm.1, f32[1,128]{1,0:T(1,128)} %bitcast.13, f32[1,128]{1,0:T(1,128)} %bitcast.14, ...), custom_call_target="tpu_custom_call" | custom-call | tf_op jit(solution)/shard_map/pallas_call | solution.py:554
  82.5 1.9 %copy.17 = bf16[1,128,2048]{2,1,0:T(8,128)(2,1)} copy(bf16[1,128,2048]{2,1,0:T(8,128)(2,1)} %bitcast.9) | data formatting | bytes 1048576
  (2 shorter events, 0.0 us)
Async XLA Ops:
  0.0 0.7 copy-start
where the time goes:
time: 84.7 us; the launch traced here: 84.4 us
  Pallas kernels  81 us (96%)
  local copies, waits for them, and re-layouts  3.28 us (4%)
    pallas_call x1, Pallas kernels, layer_device(): pl.pallas_call(layer_kernel, out_shape=jax.ShapeDtypeStruct((rows, 2 * co...  81 us
    unnamed x3, local copies, waits for them, and re-layouts  2.57 us

commit v1 on v0

--- a/solution.py
+++ b/solution.py
@@ -26,24 +26,19 @@
     seqlen = projected.shape[1]
     heads = projected.shape[2] // HD
     ntiles = seqlen // TILE
-    ktiles = table.shape[1]
     queries = rms_norm(projected[0].reshape(seqlen, heads, HD), query_gain)
     keys = rms_norm(projected[1].reshape(seqlen, heads, HD), key_gain)
     values = projected[2].reshape(seqlen, heads, HD).astype(jnp.bfloat16)
-    query_tiles = queries.reshape(ntiles, TILE, heads, HD)
-    key_sel = jnp.take(keys.reshape(ntiles, TILE, heads, HD), table, axis=0).reshape(
-        ntiles, ktiles * TILE, heads, HD
-    )
-    value_sel = jnp.take(values.reshape(ntiles, TILE, heads, HD), table, axis=0).reshape(
-        ntiles, ktiles * TILE, heads, HD
-    )
+    member = jnp.any(table[:, :, None] == jnp.arange(ntiles, dtype=table.dtype), axis=1)
+    seen = jnp.repeat(jnp.repeat(member, TILE, axis=0), TILE, axis=1)
     scores = jnp.einsum(
-        "nqhd,nkhd->nhqk", query_tiles, key_sel, preferred_element_type=jnp.float32
+        "qhd,khd->hqk", queries, keys, preferred_element_type=jnp.float32
     ) * HD ** (-0.5)
+    scores = jnp.where(seen[None], scores, MASKED)
     largest = jnp.max(scores, axis=-1, keepdims=True)
     expo = jnp.exp(scores - largest)
     weights = (expo / jnp.sum(expo, axis=-1, keepdims=True)).astype(jnp.bfloat16)
-    result = jnp.einsum("nhqk,nkhd->nqhd", weights, value_sel, preferred_element_type=jnp.float32)
+    result = jnp.einsum("hqk,khd->qhd", weights, values, preferred_element_type=jnp.float32)
     return result.astype(jnp.bfloat16).reshape(seqlen, heads * HD)
 
 

time: 84.7 us -> 84.7 us (level)
  no operation moved by 1% of the time
where the time goes in v1:
time: 84.7 us; the launch traced here: 84.4 us
  Pallas kernels  81 us (96%)
  local copies, waits for them, and re-layouts  3.28 us (4%)
    pallas_call x1, Pallas kernels, layer_device(): pl.pallas_call(layer_kernel, out_shape=jax.ShapeDtypeStruct((rows, 2 * co...  81 us
    unnamed x3, local copies, waits for them, and re-layouts  2.57 us

profile of v1, /device:TPU:3, one launch (start us, length us, event | category | flops | bytes accessed | tf_op | source)
XLA Modules:
  0.0 84.4 jit_solution(4638987341772544231)
XLA Ops:
  0.0 0.0 copy-start
  0.0 0.7 copy-done
  0.7 0.1 constant_dynamic-slice_fusion
  0.8 0.1 fusion
  0.9 0.6 broadcast_in_dim.14
  1.5 81.0 %shard_map.82 = bf16[128,2048]{1,0:T(8,128)(2,1)} custom-call(bf16[128,3072]{1,0:T(8,128)(2,1)} %bitcast.10, f32[1,3072]{1,0:T(1,128)} %shift_hbm.1, f32[1,3072]{1,0:T(1,128)} %scale_hbm.1, bf16[128,128]{1,0:T(8,128)(2,1)} %bitcast.11, f32[3,1024]{1,0:T(4,128)} %bias_hbm.1, f32[1,128]{1,0:T(1,128)} %bitcast.13, f32[1,128]{1,0:T(1,128)} %bitcast.14, ...), custom_call_target="tpu_custom_call" | custom-call | tf_op jit(solution)/shard_map/pallas_call | solution.py:549
  82.5 1.9 %copy.17 = bf16[1,128,2048]{2,1,0:T(8,128)(2,1)} copy(bf16[1,128,2048]{2,1,0:T(8,128)(2,1)} %bitcast.9) | data formatting | bytes 1048576
  (2 shorter events, 0.0 us)
Async XLA Ops:
  0.0 0.7 copy-start

commit v2 on v1

--- a/solution.py
+++ b/solution.py
@@ -7,7 +7,6 @@
 
 HD = 128
 TILE = 16
-LANES = 128
 
 
 EPS = 1e-06
@@ -66,10 +65,10 @@
     video_hbm,
     shift_hbm,
     scale_hbm,
-    member_ref,
     bias_hbm,
     qgain_hbm,
     kgain_hbm,
+    table_hbm,
     weight_ref,
     out_ref,
     video_ref,
@@ -78,8 +77,10 @@
     bias_ref,
     qgain_ref,
     kgain_ref,
+    table_ref,
     wbuf,
     tok,
+    member,
     obuf,
     own_sem,
     small_sem,
@@ -88,6 +89,8 @@
     wrecv,
     tsend,
     trecv,
+    msend,
+    mrecv,
     osend,
     orecv,
 ):
@@ -122,6 +125,7 @@
                 (bias_hbm, bias_ref),
                 (qgain_hbm, qgain_ref),
                 (kgain_hbm, kgain_ref),
+                (table_hbm, table_ref),
             ]
         )
     ]
@@ -273,11 +277,7 @@
             shifted = tokens - centre
             spread = jnp.mean(shifted * shifted, axis=-1, keepdims=True)
             normed = shifted * lax.rsqrt(spread + EPS) * (1.0 + scale_ref[...]) + shift_ref[...]
-            tok[0, pos(0), pl.ds(half + first, step), 0:width] = normed.astype(jnp.bfloat16)
-
-        tok[0, pos(0), pl.ds(half, part), width : width + LANES] = member_ref[
-            q * part : (q + 1) * part, :
-        ]
+            tok[0, pos(0), pl.ds(half + first, step), :] = normed.astype(jnp.bfloat16)
 
     def tokens_at(group, place, side, q):
         first = pl.multiple_of(side * rows + q * part, TILE)
@@ -341,9 +341,44 @@
                     wait_tokens(group, place, side, q)
 
     total = 2 * rows
-    spread_tiles = (
-        lax.broadcasted_iota(jnp.int32, (LANES, total), 1) // TILE
-        == lax.broadcasted_iota(jnp.int32, (LANES, total), 0)
+    slots, _, tiles = table_ref.shape
+
+    def write_member():
+        key_tile = lax.broadcasted_iota(jnp.int32, (tiles, tiles), 0)
+        held = key_tile == table_ref[0]
+        for n in range(1, slots):
+            held = jnp.logical_or(held, key_tile == table_ref[n])
+        member[0, pos(0)] = held.astype(jnp.float32).astype(jnp.bfloat16)
+
+    def member_send(n, group, target):
+        return remote(
+            member.at[0, pos(0)],
+            member.at[group, pos(0)],
+            msend.at[n],
+            mrecv.at[group, pos(0)],
+            target,
+        )
+
+    def member_sends(role):
+        sends = [member_send(k - 1, 0, at(k)) for k in (1, 2, 3)]
+        if role == "end":
+            sends += [member_send(3 + k, 1, at(k, 0, mate)) for k in range(4)]
+        return sends
+
+    def wait_members(group):
+        for k in range(4):
+            if k or group:
+                remote(
+                    member.at[group, pos(k)],
+                    member.at[group, pos(k)],
+                    msend.at[0],
+                    mrecv.at[group, pos(k)],
+                    at(1),
+                ).wait_recv()
+
+    in_tile = (
+        lax.broadcasted_iota(jnp.int32, (total, tiles), 0) // TILE
+        == lax.broadcasted_iota(jnp.int32, (total, tiles), 1)
     ).astype(jnp.bfloat16)
 
     def out_copy(group, h, v, side):
@@ -356,7 +391,7 @@
         )
 
     def attend(group, h, v):
-        normed = tok[group, v, :, 0:width]
+        normed = tok[group, v]
         acc = jnp.dot(normed, wbuf[h], preferred_element_type=jnp.float32)
         place = columns(pos(0), h)
         query = acc[:, 0:HD] + bias_ref[0:1, place]
@@ -367,11 +402,11 @@
         scores = lax.dot_general(
             queries, keys, (((1,), (1,)), ((), ())), preferred_element_type=jnp.float32
         ) * HD ** (-0.5)
-        seen = jnp.dot(
-            tok[group, v, :, width : width + LANES],
-            spread_tiles,
-            preferred_element_type=jnp.float32,
-        )
+        both = (((1,), (1,)), ((), ()))
+        rows_seen = lax.dot_general(
+            in_tile, member[group, v], both, preferred_element_type=jnp.float32
+        ).astype(jnp.bfloat16)
+        seen = lax.dot_general(rows_seen, in_tile, both, preferred_element_type=jnp.float32)
         scores = jnp.where(seen > 0.5, scores, MASKED)
         largest = jnp.max(scores, axis=-1, keepdims=True)
         expo = jnp.exp(scores - largest)
@@ -453,15 +488,18 @@
             copies[1].start()
 
     norm_and_send(0, CHUNKS // 2)
+    write_member()
 
     @pl.when(end)
     def _():
+        start(member_sends("end"))
         own_layer(0, (2, 3), "end")
         for q in range(CHUNKS // 2):
             end_tokens(q)[0].start()
 
     @pl.when(inner)
     def _():
+        start(member_sends("inner"))
         own_layer(0, (2, 3), "inner")
 
     norm_and_send(CHUNKS // 2, CHUNKS)
@@ -482,10 +520,12 @@
         relay(0, [3 - mate], "end")
         relay(0, [3 - z], "end")
         wait_sibling_tokens(0)
+        wait_members(0)
         attend_all(0, 0)
         outs_received(0, False)
         outs_received(1, True)
         outs_sent(0, 0)
+        sent(member_sends("end"))
         for q in chunks:
             sent(own_tokens(q) + passed_tokens(q) + end_tokens(q))
         for h in range(2):
@@ -506,6 +546,7 @@
             passed_tokens(q)[3].start()
         relay(1, [far], "inner")
         wait_sibling_tokens(0)
+        wait_members(0)
         attend_all(0, 0)
         for q in chunks:
             wait_tokens(1, *beside, q)
@@ -519,11 +560,13 @@
             wait_tokens(1, *diagonal, q)
             copies[5].start()
         wait_sibling_tokens(1)
+        wait_members(1)
         attend_all(1, 1)
         for h in range(2):
             outs_received(h, False)
             outs_sent(0, h)
         outs_sent(1, 1)
+        sent(member_sends("inner"))
         for q in chunks:
             sent(own_tokens(q) + passed_tokens(q) + shared_tokens(q))
         for layer in (z, far, peer, far_peer):
@@ -538,38 +581,39 @@
 def layer_device(video, shift, scale, project_weight, project_bias, query_gain, key_gain, tile_table):
     rows, width = video.shape[1:]
     slab, columns = project_weight.shape[1:]
-    tiles = rows // TILE
-    table = lax.dynamic_slice_in_dim(tile_table[0], lax.axis_index("seq") * tiles, tiles, 0)
-    member = jnp.any(table[:, :, None] == jnp.arange(LANES, dtype=jnp.int32), axis=1)
-    member = jnp.repeat(member.astype(jnp.bfloat16), TILE, axis=0)
+    table = jnp.transpose(tile_table, (2, 0, 1))
+    tiles = table.shape[2]
     vmem = pl.BlockSpec(memory_space=pltpu.VMEM)
     anywhere = pl.BlockSpec(memory_space=pl.ANY)
     dma = pltpu.SemaphoreType.DMA
-    small = (video[0], shift, scale, project_bias, query_gain[None], key_gain[None])
+    small = (video[0], shift, scale, project_bias, query_gain[None], key_gain[None], table)
     out = pl.pallas_call(
         layer_kernel,
         out_shape=jax.ShapeDtypeStruct((rows, 2 * columns), jnp.bfloat16),
-        in_specs=[anywhere] * 3 + [vmem] + [anywhere] * 4,
+        in_specs=[anywhere] * 8,
         out_specs=vmem,
         scratch_shapes=[pltpu.VMEM(array.shape, array.dtype) for array in small]
         + [
             pltpu.VMEM((2, 16 * slab, 3 * HD), jnp.bfloat16),
-            pltpu.VMEM((2, 4, 2 * rows, width + LANES), jnp.bfloat16),
+            pltpu.VMEM((2, 4, 2 * rows, width), jnp.bfloat16),
+            pltpu.VMEM((2, 4, tiles, tiles), jnp.bfloat16),
             pltpu.VMEM((3, 4, 2 * rows, HD), jnp.bfloat16),
             dma((2,)),
-            dma((6,)),
+            dma((7,)),
             dma((2, 3, 3)),
             dma((2, 16, 2)),
             dma((2, 16)),
             dma((2, 8, CHUNKS)),
             dma((2, 4, 2, CHUNKS)),
+            dma((7,)),
+            dma((2, 4)),
             dma((3, 4, 2)),
             dma((2, 2, 4)),
         ],
         compiler_params=pltpu.CompilerParams(
             collective_id=0, has_side_effects=True, vmem_limit_bytes=60 << 20
         ),
-    )(*small[:3], member, *small[3:], project_weight)
+    )(*small, project_weight)
     return out[None]
 
 
@@ -582,7 +626,7 @@
             and video.shape[0] == 1
             and project_weight.shape[2] == 8 * HD
             and video.shape[1] % (CHUNKS * TILE) == 0
-            and 2 * video.shape[1] // TILE <= LANES
+            and operands[7].shape[1] == 2 * video.shape[1] // TILE
             and video.shape[1] <= 256
         )
         if fits:

time: 84.7 us -> 81.3 us (0.960)
  Pallas kernels: 81 us -> 78.9 us
  local copies, waits for them, and re-layouts: 3.28 us -> 1.88 us
    pallas_call x1, Pallas kernels: 81 us -> 78.9 us  [layer_device(): pl.pallas_call(layer_kernel, out_shape=jax.ShapeDtypeStruct((rows, 2 * co...]
    unnamed x3 -> x1, local copies, waits for them, and re-layouts: 2.57 us -> 1.88 us
where the time goes in v2:
time: 81.3 us; the launch traced here: 80.8 us
  Pallas kernels  78.9 us (97%)
  local copies, waits for them, and re-layouts  1.88 us (2%)
    pallas_call x1, Pallas kernels, layer_device(): pl.pallas_call(layer_kernel, out_shape=jax.ShapeDtypeStruct((rows, 2 * co...  78.9 us
    unnamed x1, local copies, waits for them, and re-layouts  1.88 us

profile of v2, /device:TPU:3, one launch (start us, length us, event | category | flops | bytes accessed | tf_op | source)
XLA Modules:
  0.0 80.8 jit_solution(18194015760751238806)
XLA Ops:
  0.0 78.9 %shard_map.82 = bf16[128,2048]{1,0:T(8,128)(2,1)} custom-call(bf16[128,3072]{1,0:T(8,128)(2,1)} %bitcast.6, f32[1,3072]{1,0:T(1,128)} %shift_hbm.1, f32[1,3072]{1,0:T(1,128)} %scale_hbm.1, f32[3,1024]{1,0:T(4,128)} %bias_hbm.1, f32[1,128]{1,0:T(1,128)} %bitcast.8, f32[1,128]{1,0:T(1,128)} %bitcast.9, s32[12,1,16]{2,1,0:T(1,128)} %bitcast.7, ...), custom_call_target="tpu_custom_call" | custom-call | tf_op jit(solution)/shard_map/pallas_call | solution.py:590
  78.9 1.9 %copy.10 = bf16[1,128,2048]{2,1,0:T(8,128)(2,1)} copy(bf16[1,128,2048]{2,1,0:T(8,128)(2,1)} %bitcast.5) | data formatting | bytes 1048576

commit v3 on v2

--- a/solution.py
+++ b/solution.py
@@ -89,6 +89,7 @@
     wrecv,
     tsend,
     trecv,
+    srecv,
     msend,
     mrecv,
     osend,
@@ -195,7 +196,7 @@
             remote(
                 weight_ref.at[i, :, columns(pos(k), h)],
                 wbuf.at[h, mine, pl.ds(i * HD, HD)],
-                wsend.at[h, k - 1, i],
+                wsend.at[h, k - 1],
                 wrecv.at[h, dp],
                 at(k),
             )
@@ -206,14 +207,14 @@
         return remote(
             block(h, owner),
             block(h, owner),
-            zsend.at[h, owner, way],
+            zsend.at[way],
             wrecv.at[h, owner],
             at(0, 0, layer),
         )
 
     def wait_block(h, owner):
         remote(
-            block(h, owner), block(h, owner), zsend.at[h, owner, 0], wrecv.at[h, owner], at(1)
+            block(h, owner), block(h, owner), zsend.at[0], wrecv.at[h, owner], at(1)
         ).wait_recv()
 
     def wait_own(h, k):
@@ -267,7 +268,7 @@
     part = rows // CHUNKS
 
     def norm_chunk(q):
-        half = pl.multiple_of(y * rows + q * part, TILE)
+        half = pl.multiple_of((pos(0) * 2 + y) * rows + q * part, TILE)
 
         @pl.loop(0, part // step)
         def _(n):
@@ -277,24 +278,42 @@
             shifted = tokens - centre
             spread = jnp.mean(shifted * shifted, axis=-1, keepdims=True)
             normed = shifted * lax.rsqrt(spread + EPS) * (1.0 + scale_ref[...]) + shift_ref[...]
-            tok[0, pos(0), pl.ds(half + first, step), :] = normed.astype(jnp.bfloat16)
+            tok[pl.ds(half + first, step), :] = normed.astype(jnp.bfloat16)
 
     def tokens_at(group, place, side, q):
-        first = pl.multiple_of(side * rows + q * part, TILE)
-        return tok.at[group, place, pl.ds(first, part), :]
-
-    def token_send(n, group, place, side, q, target, to_group=None):
+        first = (group * 8 + place * 2 + side) * rows + q * part
+        return tok.at[pl.ds(pl.multiple_of(first, TILE), part), :]
+
+    def token_send(group, place, side, q, target, to_group=None):
         to_group = group if to_group is None else to_group
         return remote(
             tokens_at(group, place, side, q),
             tokens_at(to_group, place, side, q),
-            tsend.at[to_group, n, q],
-            trecv.at[to_group, place, side, q],
+            tsend,
+            trecv.at[to_group, place // 2, side, q],
             target,
         )
 
+    def sibling_send(group, place, side, q):
+        return remote(
+            tokens_at(group, place, side, q),
+            tokens_at(group, place, side, q),
+            tsend,
+            srecv.at[group, place // 2, side],
+            at(1),
+        )
+
     def wait_tokens(group, place, side, q):
-        token_send(0, group, place, side, q, at(1)).wait_recv()
+        token_send(group, place, side, q, at(1)).wait_recv()
+
+    def wait_sibling_tokens(group):
+        for place in (pos(1), pos(3)):
+            for side in range(2):
+                first = (group * 8 + place * 2 + side) * rows
+                extent = tok.at[pl.ds(pl.multiple_of(first, TILE), rows), :]
+                remote(
+                    extent, extent, tsend, srecv.at[group, place // 2, side], at(1)
+                ).wait_recv()
 
     own, beside, across, diagonal = (
         (pos(0), y),
@@ -305,40 +324,34 @@
 
     def own_tokens(q):
         return [
-            token_send(0, 0, *own, q, at(2)),
-            token_send(1, 0, *own, q, at(0, 1)),
-            token_send(2, 0, *own, q, at(1)),
+            token_send(0, *own, q, at(2)),
+            token_send(0, *own, q, at(0, 1)),
+            sibling_send(0, *own, q),
         ]
 
     def passed_tokens(q):
         return [
-            token_send(3, 0, *beside, q, at(0, 1)),
-            token_send(4, 0, *beside, q, at(1)),
-            token_send(5, 0, *across, q, at(1)),
-            token_send(6, 0, *diagonal, q, at(1)),
+            token_send(0, *beside, q, at(0, 1)),
+            sibling_send(0, *beside, q),
+            sibling_send(0, *across, q),
+            sibling_send(0, *diagonal, q),
         ]
 
     def end_tokens(q):
         return [
-            token_send(6, 0, *own, q, at(0, 0, mate), 1),
-            token_send(7, 0, *diagonal, q, at(0, 0, mate), 1),
+            token_send(0, *own, q, at(0, 0, mate), 1),
+            token_send(0, *diagonal, q, at(0, 0, mate), 1),
         ]
 
     def shared_tokens(q):
         return [
-            token_send(0, 1, *own, q, at(2)),
-            token_send(1, 1, *own, q, at(0, 1)),
-            token_send(2, 1, *own, q, at(1)),
-            token_send(3, 1, *beside, q, at(1)),
-            token_send(4, 1, *across, q, at(1)),
-            token_send(5, 1, *diagonal, q, at(1)),
+            token_send(1, *own, q, at(2)),
+            token_send(1, *own, q, at(0, 1)),
+            sibling_send(1, *own, q),
+            sibling_send(1, *beside, q),
+            sibling_send(1, *across, q),
+            sibling_send(1, *diagonal, q),
         ]
-
-    def wait_sibling_tokens(group):
-        for place in (pos(1), pos(3)):
-            for side in (y, 1 - y):
-                for q in range(CHUNKS):
-                    wait_tokens(group, place, side, q)
 
     total = 2 * rows
     slots, _, tiles = table_ref.shape
@@ -348,50 +361,47 @@
         held = key_tile == table_ref[0]
         for n in range(1, slots):
             held = jnp.logical_or(held, key_tile == table_ref[n])
-        member[0, pos(0)] = held.astype(jnp.float32).astype(jnp.bfloat16)
-
-    def member_send(n, group, target):
+        member[pos(0)] = held.astype(jnp.float32).astype(jnp.bfloat16)
+
+    def member_send(group, target):
         return remote(
-            member.at[0, pos(0)],
-            member.at[group, pos(0)],
-            msend.at[n],
-            mrecv.at[group, pos(0)],
+            member.at[pos(0)],
+            member.at[group * 4 + pos(0)],
+            msend,
+            mrecv.at[group],
             target,
         )
 
     def member_sends(role):
-        sends = [member_send(k - 1, 0, at(k)) for k in (1, 2, 3)]
+        sends = [member_send(0, at(k)) for k in (1, 2, 3)]
         if role == "end":
-            sends += [member_send(3 + k, 1, at(k, 0, mate)) for k in range(4)]
+            sends += [member_send(1, at(k, 0, mate)) for k in range(4)]
         return sends
 
     def wait_members(group):
-        for k in range(4):
-            if k or group:
-                remote(
-                    member.at[group, pos(k)],
-                    member.at[group, pos(k)],
-                    msend.at[0],
-                    mrecv.at[group, pos(k)],
-                    at(1),
-                ).wait_recv()
+        extent = member.at[pl.ds(0, 3 + group)]
+        remote(extent, extent, msend, mrecv.at[group], at(1)).wait_recv()
 
     in_tile = (
         lax.broadcasted_iota(jnp.int32, (total, tiles), 0) // TILE
         == lax.broadcasted_iota(jnp.int32, (total, tiles), 1)
     ).astype(jnp.bfloat16)
 
+    def results_at(group, h, v, side, size):
+        first = ((group + h) * 8 + v * 2 + side) * rows
+        return pl.ds(pl.multiple_of(first, TILE), size)
+
     def out_copy(group, h, v, side):
         return remote(
-            obuf.at[group + h, v, pl.ds(side * rows, rows), :],
+            obuf.at[results_at(group, h, v, side, rows), :],
             out_ref.at[:, columns(y * 4 + pos(0), h)],
-            osend.at[group + h, v, side],
-            orecv.at[h, y, pos(0)],
+            osend,
+            orecv,
             ((far if group else z) * 4 + v, side),
         )
 
     def attend(group, h, v):
-        normed = tok[group, v]
+        normed = tok[pl.ds(pl.multiple_of((group * 4 + v) * total, TILE), total), :]
         acc = jnp.dot(normed, wbuf[h], preferred_element_type=jnp.float32)
         place = columns(pos(0), h)
         query = acc[:, 0:HD] + bias_ref[0:1, place]
@@ -404,7 +414,7 @@
         ) * HD ** (-0.5)
         both = (((1,), (1,)), ((), ()))
         rows_seen = lax.dot_general(
-            in_tile, member[group, v], both, preferred_element_type=jnp.float32
+            in_tile, member[group * 4 + v], both, preferred_element_type=jnp.float32
         ).astype(jnp.bfloat16)
         seen = lax.dot_general(rows_seen, in_tile, both, preferred_element_type=jnp.float32)
         scores = jnp.where(seen > 0.5, scores, MASKED)
@@ -414,7 +424,7 @@
         result = jnp.dot(
             weights, value.astype(jnp.bfloat16), preferred_element_type=jnp.float32
         ).astype(jnp.bfloat16)
-        obuf[group + h, v] = result
+        obuf[results_at(group, h, v, 0, total), :] = result
         for side in range(2):
             if group:
                 out_copy(group, h, v, side).start()
@@ -434,42 +444,28 @@
         def _(v):
             attend(group, h, v)
 
-    def outs_sent(group, h):
-        for v in range(4):
-            for side in range(2):
-                if group:
-                    out_copy(group, h, v, side).wait_send()
-                    continue
-
-                @pl.when(jnp.logical_or(v != pos(0), side != y))
-                def _():
-                    out_copy(group, h, v, side).wait_send()
-
-    def outs_received(h, whole):
-        for flip in range(2):
-            for k in range(4):
-                if k or flip or whole:
-                    side = 1 - y if flip else y
-                    remote(
-                        obuf.at[h, 0, pl.ds(0, rows), :],
-                        out_ref.at[:, columns(side * 4 + pos(k), h)],
-                        osend.at[h, 0, 0],
-                        orecv.at[h, side, pos(k)],
-                        at(1),
-                    ).wait_recv()
-
-    def z_sent(h, layer, role):
-        for k in range(4):
-            for way, target in ways(h, layer, role):
-                z_send(h, layer * 4 + pos(k), way, target).wait_send()
+    def bytes_sent(array, count, sem):
+        extent = array.at[pl.ds(0, count)]
+        remote(extent, extent, sem, sem, at(1)).wait_send()
+
+    def all_sent(z_blocks, half_videos, members, results):
+        for way, blocks in enumerate(z_blocks):
+            if blocks:
+                bytes_sent(wbuf.at[0], blocks * slab, zsend.at[way])
+        bytes_sent(tok, half_videos * rows, tsend)
+        bytes_sent(member, members, msend)
+        bytes_sent(obuf, results * rows, osend)
+        for h in range(2):
+            for k in (1, 2, 3):
+                bytes_sent(wbuf.at[0], slab, wsend.at[h, k - 1])
+
+    def outs_received(count):
+        extent = out_ref.at[:, 0 : count * HD]
+        remote(extent, extent, osend, orecv, at(1)).wait_recv()
 
     def start(copies):
         for copy in copies:
             copy.start()
-
-    def sent(copies):
-        for copy in copies:
-            copy.wait_send()
 
     chunks = range(CHUNKS)
 
@@ -522,14 +518,8 @@
         wait_sibling_tokens(0)
         wait_members(0)
         attend_all(0, 0)
-        outs_received(0, False)
-        outs_received(1, True)
-        outs_sent(0, 0)
-        sent(member_sends("end"))
-        for q in chunks:
-            sent(own_tokens(q) + passed_tokens(q) + end_tokens(q))
-        for h in range(2):
-            z_sent(h, z, "end")
+        outs_received(15)
+        all_sent((8, 0), 9, 7, 7)
 
     @pl.when(inner)
     def _():
@@ -562,20 +552,8 @@
         wait_sibling_tokens(1)
         wait_members(1)
         attend_all(1, 1)
-        for h in range(2):
-            outs_received(h, False)
-            outs_sent(0, h)
-        outs_sent(1, 1)
-        sent(member_sends("inner"))
-        for q in chunks:
-            sent(own_tokens(q) + passed_tokens(q) + shared_tokens(q))
-        for layer in (z, far, peer, far_peer):
-            for h in range(2):
-                z_sent(h, layer, "inner")
-
-    for h in range(2):
-        for k in (1, 2, 3):
-            sent(piece_sends(h, k))
+        outs_received(14)
+        all_sent((12, 16), 13, 3, 22)
 
 
 def layer_device(video, shift, scale, project_weight, project_bias, query_gain, key_gain, tile_table):
@@ -589,26 +567,27 @@
     small = (video[0], shift, scale, project_bias, query_gain[None], key_gain[None], table)
     out = pl.pallas_call(
         layer_kernel,
-        out_shape=jax.ShapeDtypeStruct((rows, 2 * columns), jnp.bfloat16),
+        out_shape=pltpu.VMEM((rows, 2 * columns), jnp.bfloat16),
         in_specs=[anywhere] * 8,
         out_specs=vmem,
         scratch_shapes=[pltpu.VMEM(array.shape, array.dtype) for array in small]
         + [
             pltpu.VMEM((2, 16 * slab, 3 * HD), jnp.bfloat16),
-            pltpu.VMEM((2, 4, 2 * rows, width), jnp.bfloat16),
-            pltpu.VMEM((2, 4, tiles, tiles), jnp.bfloat16),
-            pltpu.VMEM((3, 4, 2 * rows, HD), jnp.bfloat16),
+            pltpu.VMEM((16 * rows, width), jnp.bfloat16),
+            pltpu.VMEM((8, tiles, tiles), jnp.bfloat16),
+            pltpu.VMEM((24 * rows, HD), jnp.bfloat16),
             dma((2,)),
             dma((7,)),
-            dma((2, 3, 3)),
-            dma((2, 16, 2)),
+            dma((2, 3)),
+            dma((2,)),
             dma((2, 16)),
-            dma((2, 8, CHUNKS)),
-            dma((2, 4, 2, CHUNKS)),
-            dma((7,)),
-            dma((2, 4)),
-            dma((3, 4, 2)),
-            dma((2, 2, 4)),
+            dma,
+            dma((2, 2, 2, CHUNKS)),
+            dma((2, 2, 2)),
+            dma,
+            dma((2,)),
+            dma,
+            dma,
         ],
         compiler_params=pltpu.CompilerParams(
             collective_id=0, has_side_effects=True, vmem_limit_bytes=60 << 20

time: 81.3 us -> 77.8 us (0.957)
  Pallas kernels: 78.9 us -> 76.6 us
  local copies, waits for them, and re-layouts: 1.88 us -> 0.8 us
    pallas_call x1, Pallas kernels: 78.9 us -> 76.6 us  [layer_device(): pl.pallas_call(layer_kernel, out_shape=pltpu.VMEM((rows, 2 * columns), jn...]
    unnamed x1, local copies, waits for them, and re-layouts: 1.88 us -> 0.8 us
where the time goes in v3:
time: 77.8 us; the launch traced here: 77.4 us
  Pallas kernels  76.6 us (98%)
  local copies, waits for them, and re-layouts  0.8 us (1%)
    pallas_call x1, Pallas kernels, layer_device(): pl.pallas_call(layer_kernel, out_shape=pltpu.VMEM((rows, 2 * columns), jn...  76.6 us

profile of v3, /device:TPU:3, one launch (start us, length us, event | category | flops | bytes accessed | tf_op | source)
XLA Modules:
  0.0 77.4 jit_solution(15424357088962716926)
XLA Ops:
  0.0 76.6 %shard_map.82 = bf16[128,2048]{1,0:T(8,128)(2,1)S(1)} custom-call(bf16[128,3072]{1,0:T(8,128)(2,1)} %bitcast.6, f32[1,3072]{1,0:T(1,128)} %shift_hbm.1, f32[1,3072]{1,0:T(1,128)} %scale_hbm.1, f32[3,1024]{1,0:T(4,128)} %bias_hbm.1, f32[1,128]{1,0:T(1,128)} %bitcast.8, f32[1,128]{1,0:T(1,128)} %bitcast.9, s32[12,1,16]{2,1,0:T(1,128)} %bitcast.7, ...), custom_call_target="tpu_custom_call" | custom-call | tf_op jit(solution)/shard_map/pallas_call | solution.py:568
  76.6 0.8 %copy.10 = bf16[1,128,2048]{2,1,0:T(8,128)(2,1)} copy(bf16[1,128,2048]{2,1,0:T(8,128)(2,1)S(1)} %bitcast.5) | data formatting | bytes 1048576

commit v4 on v3

--- a/solution.py
+++ b/solution.py
@@ -11,7 +11,7 @@
 
 EPS = 1e-06
 MASKED = -1e30
-CHUNKS = 2
+CHUNKS = 4
 MESH = pl.DeviceIdType.MESH
 
 
@@ -81,6 +81,8 @@
     wbuf,
     tok,
     member,
+    masks,
+    accs,
     obuf,
     own_sem,
     small_sem,
@@ -306,14 +308,10 @@
     def wait_tokens(group, place, side, q):
         token_send(group, place, side, q, at(1)).wait_recv()
 
-    def wait_sibling_tokens(group):
-        for place in (pos(1), pos(3)):
-            for side in range(2):
-                first = (group * 8 + place * 2 + side) * rows
-                extent = tok.at[pl.ds(pl.multiple_of(first, TILE), rows), :]
-                remote(
-                    extent, extent, tsend, srecv.at[group, place // 2, side], at(1)
-                ).wait_recv()
+    def wait_sibling_tokens(group, k, side):
+        first = (group * 8 + pos(k) * 2 + side) * rows
+        extent = tok.at[pl.ds(pl.multiple_of(first, TILE), rows), :]
+        remote(extent, extent, tsend, srecv.at[group, pos(k) // 2, side], at(1)).wait_recv()
 
     own, beside, across, diagonal = (
         (pos(0), y),
@@ -351,6 +349,7 @@
             sibling_send(1, *beside, q),
             sibling_send(1, *across, q),
             sibling_send(1, *diagonal, q),
+            token_send(1, *across, q, at(2)),
         ]
 
     total = 2 * rows
@@ -400,59 +399,89 @@
             ((far if group else z) * 4 + v, side),
         )
 
-    def attend(group, h, v):
-        normed = tok[pl.ds(pl.multiple_of((group * 4 + v) * total, TILE), total), :]
-        acc = jnp.dot(normed, wbuf[h], preferred_element_type=jnp.float32)
+    both = (((1,), (1,)), ((), ()))
+
+    def write_masks(group):
+        for v in range(4):
+            rows_seen = lax.dot_general(
+                in_tile, member[group * 4 + v], both, preferred_element_type=jnp.float32
+            ).astype(jnp.bfloat16)
+            seen = lax.dot_general(rows_seen, in_tile, both, preferred_element_type=jnp.float32)
+            masks[group * 4 + v] = jnp.where(seen > 0.5, 0.0, MASKED)
+
+    most = (jnp.where(z == 1, 0, 4 * slab), 12 * slab)
+    last = (far_peer * 4 * slab, 4 * slab)
+    whole = (0, 16 * slab)
+
+    def project(first, size, h, depth, add=False):
+        row = pl.ds(pl.multiple_of(first, TILE), size)
+        inner_rows = pl.ds(pl.multiple_of(depth[0], HD), depth[1])
+        part = jnp.dot(
+            tok[row, inner_rows], wbuf[h, inner_rows, :], preferred_element_type=jnp.float32
+        )
+        accs[row, :] = accs[row, :] + part if add else part
+
+    def project_pair(group, h, k, depth, add=False):
+        project((group * 4 + pos(k) // 2 * 2) * total, 2 * total, h, depth, add)
+
+    def project_sides(group, h, k, side, depth, add=False):
+        for m in range(2):
+            video = group * 4 + pos(k) // 2 * 2 + m
+            project((video * 2 + side) * rows, rows, h, depth, add)
+
+    def attend(group, h, k):
+        first = pos(k) // 2 * 2
+        pair = pl.ds(pl.multiple_of((group * 4 + first) * total, TILE), 2 * total)
+        acc = accs[pair, :]
         place = columns(pos(0), h)
         query = acc[:, 0:HD] + bias_ref[0:1, place]
         key = acc[:, HD : 2 * HD] + bias_ref[1:2, place]
-        value = acc[:, 2 * HD : 3 * HD] + bias_ref[2:3, place]
+        values = (acc[:, 2 * HD : 3 * HD] + bias_ref[2:3, place]).astype(jnp.bfloat16)
         queries = rms_norm(query, qgain_ref[...])
         keys = rms_norm(key, kgain_ref[...])
-        scores = lax.dot_general(
-            queries, keys, (((1,), (1,)), ((), ())), preferred_element_type=jnp.float32
-        ) * HD ** (-0.5)
-        both = (((1,), (1,)), ((), ()))
-        rows_seen = lax.dot_general(
-            in_tile, member[group * 4 + v], both, preferred_element_type=jnp.float32
-        ).astype(jnp.bfloat16)
-        seen = lax.dot_general(rows_seen, in_tile, both, preferred_element_type=jnp.float32)
-        scores = jnp.where(seen > 0.5, scores, MASKED)
-        largest = jnp.max(scores, axis=-1, keepdims=True)
-        expo = jnp.exp(scores - largest)
-        weights = (expo / jnp.sum(expo, axis=-1, keepdims=True)).astype(jnp.bfloat16)
-        result = jnp.dot(
-            weights, value.astype(jnp.bfloat16), preferred_element_type=jnp.float32
-        ).astype(jnp.bfloat16)
-        obuf[results_at(group, h, v, 0, total), :] = result
-        for side in range(2):
-            if group:
-                out_copy(group, h, v, side).start()
-                continue
-            away = jnp.logical_or(v != pos(0), side != y)
-
-            @pl.when(away)
-            def _():
-                out_copy(group, h, v, side).start()
-
-            @pl.when(jnp.logical_not(away))
-            def _():
-                out_ref[:, columns(y * 4 + pos(0), h)] = result[side * rows : (side + 1) * rows, :]
-
-    def attend_all(group, h):
-        @pl.loop(0, 4)
-        def _(v):
-            attend(group, h, v)
+        videos = [slice(m * total, (m + 1) * total) for m in range(2)]
+        scores = [
+            lax.dot_general(
+                queries[video], keys[video], both, preferred_element_type=jnp.float32
+            ) * HD ** (-0.5)
+            + masks[group * 4 + first + m]
+            for m, video in enumerate(videos)
+        ]
+        largest = [jnp.max(one, axis=-1, keepdims=True) for one in scores]
+        expo = [jnp.exp(one - top) for one, top in zip(scores, largest)]
+        weights = [
+            (one / jnp.sum(one, axis=-1, keepdims=True)).astype(jnp.bfloat16) for one in expo
+        ]
+        results = [
+            jnp.dot(one, values[video], preferred_element_type=jnp.float32).astype(jnp.bfloat16)
+            for one, video in zip(weights, videos)
+        ]
+        for m in range(2):
+            obuf[results_at(group, h, first + m, 0, total), :] = results[m]
+        for m in range(2):
+            for side in range(2):
+                copy = out_copy(group, h, first + m, side)
+                if group or k:
+                    copy.start()
+                    continue
+                away = jnp.logical_or(m != core, side != y)
+                pl.when(away)(copy.start)
+
+                @pl.when(jnp.logical_not(away))
+                def _():
+                    out_ref[:, columns(y * 4 + pos(0), h)] = results[m][
+                        side * rows : (side + 1) * rows, :
+                    ]
 
     def bytes_sent(array, count, sem):
         extent = array.at[pl.ds(0, count)]
         remote(extent, extent, sem, sem, at(1)).wait_send()
 
-    def all_sent(z_blocks, half_videos, members, results):
+    def all_sent(z_blocks, token_rows, members, results):
         for way, blocks in enumerate(z_blocks):
             if blocks:
                 bytes_sent(wbuf.at[0], blocks * slab, zsend.at[way])
-        bytes_sent(tok, half_videos * rows, tsend)
+        bytes_sent(tok, token_rows, tsend)
         bytes_sent(member, members, msend)
         bytes_sent(obuf, results * rows, osend)
         for h in range(2):
@@ -502,58 +531,105 @@
     for k in (2, 3, 1):
         start(piece_sends(1, k))
 
+    def relay_one(h, layer, k, role):
+        wait_block(h, layer * 4 + pos(k))
+        pass_on(h, layer, k, role)
+
+    def pass_tokens(group, which, q):
+        place, copies = {
+            "beside": (beside, [shared_tokens(q)[3]]),
+            "across": (across, [shared_tokens(q)[4]]),
+            "diagonal": (diagonal, [(shared_tokens(q)[5] if group else passed_tokens(q)[3])]),
+        }[which]
+        wait_tokens(group, *place, q)
+        if group and which == "across" and q == 0:
+            copies = copies + [shared_tokens(q)[6]]
+        start(copies)
+
     @pl.when(end)
     def _():
         for q in range(CHUNKS // 2, CHUNKS):
             end_tokens(q)[0].start()
         pass_direct()
         own_layer(1, range(4), "end")
-        for q in chunks:
-            wait_tokens(0, *diagonal, q)
-            end_tokens(q)[1].start()
-            passed_tokens(q)[3].start()
+        for q in (*range(1, CHUNKS), 0):
+            pass_tokens(0, "diagonal", q)
+            if q:
+                end_tokens(q)[1].start()
         relay(0, [mate], "end")
         relay(0, [3 - mate], "end")
         relay(0, [3 - z], "end")
-        wait_sibling_tokens(0)
         wait_members(0)
-        attend_all(0, 0)
+        write_masks(0)
+        for k in (0, 2):
+            for side in range(2):
+                wait_sibling_tokens(0, k + 1, side)
+            project_pair(0, 0, k, whole)
+            attend(0, 0, k)
         outs_received(15)
-        all_sent((8, 0), 9, 7, 7)
+        all_sent((8, 0), (9 * CHUNKS - 1) * part, 7, 7)
 
     @pl.when(inner)
     def _():
         relay(0, [far, peer], "inner")
         own_layer(1, (0, 1), "inner")
+        wait_members(0)
+        write_masks(0)
         pass_direct()
         relay(0, [far_peer], "inner")
         for q in chunks:
             wait_tokens(1, *own, q)
             start(shared_tokens(q)[:3])
         own_layer(1, (2, 3), "inner")
+        for side in range(2):
+            wait_sibling_tokens(0, 1, side)
+        project_pair(0, 0, 0, whole)
+        attend(0, 0, 0)
         for q in chunks:
-            wait_tokens(0, *diagonal, q)
-            passed_tokens(q)[3].start()
-        relay(1, [far], "inner")
-        wait_sibling_tokens(0)
-        wait_members(0)
-        attend_all(0, 0)
+            pass_tokens(0, "diagonal", q)
+        relay_one(1, far, 0, "inner")
+        for side in range(2):
+            wait_sibling_tokens(0, 3, side)
+        project_pair(0, 0, 2, whole)
+        attend(0, 0, 2)
+        relay_one(1, far, 1, "inner")
+        relay_one(1, far, 2, "inner")
+        pass_tokens(1, "across", 0)
+        relay_one(1, far, 3, "inner")
+        relay(1, [peer], "inner")
+        project_pair(0, 1, 0, most)
+        project_pair(0, 1, 2, most)
+        wait_members(1)
+        write_masks(1)
         for q in chunks:
-            wait_tokens(1, *beside, q)
-            shared_tokens(q)[3].start()
-        relay(1, [peer, far_peer], "inner")
-        attend_all(0, 1)
-        for q in chunks:
-            copies = shared_tokens(q)
-            wait_tokens(1, *across, q)
-            copies[4].start()
-            wait_tokens(1, *diagonal, q)
-            copies[5].start()
-        wait_sibling_tokens(1)
-        wait_members(1)
-        attend_all(1, 1)
+            pass_tokens(1, "beside", q)
+        pass_tokens(1, "across", 1)
+        wait_sibling_tokens(1, 1, y)
+        project_sides(1, 1, 0, y, most)
+        wait_sibling_tokens(1, 3, y)
+        project_sides(1, 1, 2, y, most)
+        pass_tokens(1, "across", 2)
+        relay(1, [far_peer], "inner")
+        project_pair(0, 1, 2, last, True)
+        attend(0, 1, 2)
+        project_sides(1, 1, 0, y, last, True)
+        for q in range(3, CHUNKS):
+            pass_tokens(1, "across", q)
+        for q in (1, 2, 0):
+            pass_tokens(1, "diagonal", q)
+        project_sides(1, 1, 2, y, last, True)
+        wait_sibling_tokens(1, 1, 1 - y)
+        project_sides(1, 1, 0, 1 - y, whole)
+        for q in range(3, CHUNKS):
+            pass_tokens(1, "diagonal", q)
+        attend(1, 1, 0)
+        wait_sibling_tokens(1, 3, 1 - y)
+        project_sides(1, 1, 2, 1 - y, whole)
+        attend(1, 1, 2)
+        project_pair(0, 1, 0, last, True)
+        attend(0, 1, 0)
         outs_received(14)
-        all_sent((12, 16), 13, 3, 22)
+        all_sent((12, 16), (13 * CHUNKS + 1) * part, 3, 22)
 
 
 def layer_device(video, shift, scale, project_weight, project_bias, query_gain, key_gain, tile_table):
@@ -575,6 +651,8 @@
             pltpu.VMEM((2, 16 * slab, 3 * HD), jnp.bfloat16),
             pltpu.VMEM((16 * rows, width), jnp.bfloat16),
             pltpu.VMEM((8, tiles, tiles), jnp.bfloat16),
+            pltpu.VMEM((8, 2 * rows, 2 * rows), jnp.float32),
+            pltpu.VMEM((16 * rows, 3 * HD), jnp.float32),
             pltpu.VMEM((24 * rows, HD), jnp.bfloat16),
             dma((2,)),
             dma((7,)),

time: 77.8 us -> 72.6 us (0.933)
  Pallas kernels: 76.6 us -> 70.8 us
    pallas_call x1, Pallas kernels: 76.6 us -> 70.8 us  [layer_device(): pl.pallas_call(layer_kernel, out_shape=pltpu.VMEM((rows, 2 * columns), jn...]
where the time goes in v4:
time: 72.6 us; the launch traced here: 71.6 us
  Pallas kernels  70.8 us (98%)
  local copies, waits for them, and re-layouts  0.8 us (1%)
    pallas_call x1, Pallas kernels, layer_device(): pl.pallas_call(layer_kernel, out_shape=pltpu.VMEM((rows, 2 * columns), jn...  70.8 us

profile of v4, /device:TPU:3, one launch (start us, length us, event | category | flops | bytes accessed | tf_op | source)
XLA Modules:
  0.0 71.6 jit_solution(8660625415381740185)
XLA Ops:
  0.0 70.8 %shard_map.82 = bf16[128,2048]{1,0:T(8,128)(2,1)S(1)} custom-call(bf16[128,3072]{1,0:T(8,128)(2,1)} %bitcast.6, f32[1,3072]{1,0:T(1,128)} %shift_hbm.1, f32[1,3072]{1,0:T(1,128)} %scale_hbm.1, f32[3,1024]{1,0:T(4,128)} %bias_hbm.1, f32[1,128]{1,0:T(1,128)} %bitcast.8, f32[1,128]{1,0:T(1,128)} %bitcast.9, s32[12,1,16]{2,1,0:T(1,128)} %bitcast.7, ...), custom_call_target="tpu_custom_call" | custom-call | tf_op jit(solution)/shard_map/pallas_call | solution.py:644
  70.8 0.8 %copy.10 = bf16[1,128,2048]{2,1,0:T(8,128)(2,1)} copy(bf16[1,128,2048]{2,1,0:T(8,128)(2,1)S(1)} %bitcast.5) | data formatting | bytes 1048576

commit v5 on v4

--- a/solution.py
+++ b/solution.py
@@ -11,7 +11,7 @@
 
 EPS = 1e-06
 MASKED = -1e30
-CHUNKS = 4
+CHUNKS = (3, 2, 2, 1)
 MESH = pl.DeviceIdType.MESH
 
 
@@ -164,6 +164,8 @@
 
     mine = pl.ds(pl.multiple_of(dp * slab, 16), slab)
 
+    for copy in small:
+        copy.start()
     for h in range(2):
         for i in range(3):
             pltpu.make_async_copy(
@@ -171,17 +173,6 @@
                 wbuf.at[h, mine, pl.ds(i * HD, HD)],
                 own_sem.at[h],
             ).start()
-        if h == 0:
-            for copy in small:
-                copy.start()
-
-    @pl.when(end)
-    def _():
-        pl.semaphore_wait(barrier, 15)
-
-    @pl.when(inner)
-    def _():
-        pl.semaphore_wait(barrier, 16)
 
     def remote(src, dst, send, recv, target):
         return pltpu.make_async_remote_copy(
@@ -252,30 +243,19 @@
                 wait_block(h, layer * 4 + pos(k))
                 pass_on(h, layer, k, role)
 
-    for k in (2, 3, 1):
-        for copy in piece_sends(0, k):
-            copy.start()
-
-    @pl.when(end)
-    def _():
-        own_layer(0, (0, 1), "end")
-
-    @pl.when(inner)
-    def _():
-        own_layer(0, (0, 1), "inner")
-
-    for copy in small:
-        copy.wait()
     step = 16
-    part = rows // CHUNKS
+    unit = rows // sum(CHUNKS)
+    chunks = range(len(CHUNKS))
+    offsets = [sum(CHUNKS[:q]) * unit for q in chunks]
+    sizes = [count * unit for count in CHUNKS]
 
     def norm_chunk(q):
-        half = pl.multiple_of((pos(0) * 2 + y) * rows + q * part, TILE)
-
-        @pl.loop(0, part // step)
+        half = pl.multiple_of((pos(0) * 2 + y) * rows + offsets[q], TILE)
+
+        @pl.loop(0, sizes[q] // step)
         def _(n):
             first = pl.multiple_of(n * step, step)
-            tokens = video_ref[pl.ds(q * part + first, step), :].astype(jnp.float32)
+            tokens = video_ref[pl.ds(offsets[q] + first, step), :].astype(jnp.float32)
             centre = jnp.mean(tokens, axis=-1, keepdims=True)
             shifted = tokens - centre
             spread = jnp.mean(shifted * shifted, axis=-1, keepdims=True)
@@ -283,8 +263,8 @@
             tok[pl.ds(half + first, step), :] = normed.astype(jnp.bfloat16)
 
     def tokens_at(group, place, side, q):
-        first = (group * 8 + place * 2 + side) * rows + q * part
-        return tok.at[pl.ds(pl.multiple_of(first, TILE), part), :]
+        first = (group * 8 + place * 2 + side) * rows + offsets[q]
+        return tok.at[pl.ds(pl.multiple_of(first, TILE), sizes[q]), :]
 
     def token_send(group, place, side, q, target, to_group=None):
         to_group = group if to_group is None else to_group
@@ -429,17 +409,16 @@
             video = group * 4 + pos(k) // 2 * 2 + m
             project((video * 2 + side) * rows, rows, h, depth, add)
 
-    def attend(group, h, k):
-        first = pos(k) // 2 * 2
-        pair = pl.ds(pl.multiple_of((group * 4 + first) * total, TILE), 2 * total)
-        acc = accs[pair, :]
+    def attend(group, h, first, count):
+        block = pl.ds(pl.multiple_of((group * 4 + first) * total, TILE), count * total)
+        acc = accs[block, :]
         place = columns(pos(0), h)
         query = acc[:, 0:HD] + bias_ref[0:1, place]
         key = acc[:, HD : 2 * HD] + bias_ref[1:2, place]
         values = (acc[:, 2 * HD : 3 * HD] + bias_ref[2:3, place]).astype(jnp.bfloat16)
         queries = rms_norm(query, qgain_ref[...])
         keys = rms_norm(key, kgain_ref[...])
-        videos = [slice(m * total, (m + 1) * total) for m in range(2)]
+        videos = [slice(m * total, (m + 1) * total) for m in range(count)]
         scores = [
             lax.dot_general(
                 queries[video], keys[video], both, preferred_element_type=jnp.float32
@@ -456,22 +435,35 @@
             jnp.dot(one, values[video], preferred_element_type=jnp.float32).astype(jnp.bfloat16)
             for one, video in zip(weights, videos)
         ]
-        for m in range(2):
+        for m in range(count):
             obuf[results_at(group, h, first + m, 0, total), :] = results[m]
-        for m in range(2):
+
+    def send_results(group, h, first, count, own_core=None):
+        for m in range(count):
             for side in range(2):
                 copy = out_copy(group, h, first + m, side)
-                if group or k:
+                if own_core is None:
                     copy.start()
                     continue
-                away = jnp.logical_or(m != core, side != y)
+                away = jnp.logical_or(m != own_core, side != y)
                 pl.when(away)(copy.start)
 
                 @pl.when(jnp.logical_not(away))
                 def _():
-                    out_ref[:, columns(y * 4 + pos(0), h)] = results[m][
-                        side * rows : (side + 1) * rows, :
+                    out_ref[:, columns(y * 4 + pos(0), h)] = obuf[
+                        results_at(group, h, first + m, side, rows), :
                     ]
+
+    def pair(k):
+        return pos(k) // 2 * 2
+
+    def attend_pair(group, h, k, send=True):
+        attend(group, h, pair(k), 2)
+        if send:
+            send_pair(group, h, k)
+
+    def send_pair(group, h, k):
+        send_results(group, h, pair(k), 2, None if group or k else core)
 
     def bytes_sent(array, count, sem):
         extent = array.at[pl.ds(0, count)]
@@ -496,8 +488,6 @@
         for copy in copies:
             copy.start()
 
-    chunks = range(CHUNKS)
-
     def norm_and_send(first, last):
         for q in range(first, last):
             norm_chunk(q)
@@ -512,22 +502,50 @@
             copies[0].start()
             copies[1].start()
 
-    norm_and_send(0, CHUNKS // 2)
+    early = len(CHUNKS) // 2
+    for copy in small:
+        copy.wait()
     write_member()
+    for q in range(early):
+        norm_chunk(q)
 
     @pl.when(end)
     def _():
-        start(member_sends("end"))
+        pl.semaphore_wait(barrier, 15)
+
+    @pl.when(inner)
+    def _():
+        pl.semaphore_wait(barrier, 16)
+
+    for k in (2, 3, 1):
+        start(piece_sends(0, k))
+
+    def first_sends(role):
+        start(member_sends(role))
+        for q in range(early):
+            start(own_tokens(q))
+        own_layer(0, (0, 1), role)
+
+    @pl.when(end)
+    def _():
+        first_sends("end")
+
+    @pl.when(inner)
+    def _():
+        first_sends("inner")
+
+    norm_and_send(early, len(CHUNKS))
+
+    @pl.when(end)
+    def _():
         own_layer(0, (2, 3), "end")
-        for q in range(CHUNKS // 2):
+        for q in chunks:
             end_tokens(q)[0].start()
 
     @pl.when(inner)
     def _():
-        start(member_sends("inner"))
         own_layer(0, (2, 3), "inner")
 
-    norm_and_send(CHUNKS // 2, CHUNKS)
     for k in (2, 3, 1):
         start(piece_sends(1, k))
 
@@ -548,11 +566,9 @@
 
     @pl.when(end)
     def _():
-        for q in range(CHUNKS // 2, CHUNKS):
-            end_tokens(q)[0].start()
         pass_direct()
         own_layer(1, range(4), "end")
-        for q in (*range(1, CHUNKS), 0):
+        for q in (*chunks[1:], 0):
             pass_tokens(0, "diagonal", q)
             if q:
                 end_tokens(q)[1].start()
@@ -565,17 +581,17 @@
             for side in range(2):
                 wait_sibling_tokens(0, k + 1, side)
             project_pair(0, 0, k, whole)
-            attend(0, 0, k)
+            attend_pair(0, 0, k)
         outs_received(15)
-        all_sent((8, 0), (9 * CHUNKS - 1) * part, 7, 7)
+        all_sent((8, 0), 9 * rows - sizes[0], 7, 7)
 
     @pl.when(inner)
     def _():
         relay(0, [far, peer], "inner")
         own_layer(1, (0, 1), "inner")
+        pass_direct()
         wait_members(0)
         write_masks(0)
-        pass_direct()
         relay(0, [far_peer], "inner")
         for q in chunks:
             wait_tokens(1, *own, q)
@@ -584,17 +600,18 @@
         for side in range(2):
             wait_sibling_tokens(0, 1, side)
         project_pair(0, 0, 0, whole)
-        attend(0, 0, 0)
+        attend_pair(0, 0, 0)
         for q in chunks:
             pass_tokens(0, "diagonal", q)
         relay_one(1, far, 0, "inner")
         for side in range(2):
             wait_sibling_tokens(0, 3, side)
         project_pair(0, 0, 2, whole)
-        attend(0, 0, 2)
+        attend_pair(0, 0, 2, send=False)
         relay_one(1, far, 1, "inner")
         relay_one(1, far, 2, "inner")
         pass_tokens(1, "across", 0)
+        send_pair(0, 0, 2)
         relay_one(1, far, 3, "inner")
         relay(1, [peer], "inner")
         project_pair(0, 1, 0, most)
@@ -611,25 +628,26 @@
         pass_tokens(1, "across", 2)
         relay(1, [far_peer], "inner")
         project_pair(0, 1, 2, last, True)
-        attend(0, 1, 2)
+        attend_pair(0, 1, 2)
         project_sides(1, 1, 0, y, last, True)
-        for q in range(3, CHUNKS):
+        for q in chunks[3:]:
             pass_tokens(1, "across", q)
-        for q in (1, 2, 0):
+        for q in (*chunks[1:], 0):
             pass_tokens(1, "diagonal", q)
+        for k in range(2):
+            if k:
+                wait_sibling_tokens(1, 1, 1 - y)
+            project(((4 + pos(k)) * 2 + 1 - y) * rows, rows, 1, whole)
+            attend(1, 1, pos(k), 1)
+            send_results(1, 1, pos(k), 1)
         project_sides(1, 1, 2, y, last, True)
-        wait_sibling_tokens(1, 1, 1 - y)
-        project_sides(1, 1, 0, 1 - y, whole)
-        for q in range(3, CHUNKS):
-            pass_tokens(1, "diagonal", q)
-        attend(1, 1, 0)
         wait_sibling_tokens(1, 3, 1 - y)
         project_sides(1, 1, 2, 1 - y, whole)
-        attend(1, 1, 2)
+        attend_pair(1, 1, 2)
         project_pair(0, 1, 0, last, True)
-        attend(0, 1, 0)
+        attend_pair(0, 1, 0)
         outs_received(14)
-        all_sent((12, 16), (13 * CHUNKS + 1) * part, 3, 22)
+        all_sent((12, 16), 13 * rows + sizes[0], 3, 22)
 
 
 def layer_device(video, shift, scale, project_weight, project_bias, query_gain, key_gain, tile_table):
@@ -660,7 +678,7 @@
             dma((2,)),
             dma((2, 16)),
             dma,
-            dma((2, 2, 2, CHUNKS)),
+            dma((2, 2, 2, len(CHUNKS))),
             dma((2, 2, 2)),
             dma,
             dma((2,)),
@@ -682,7 +700,7 @@
             and mesh.shape["seq"] == 2
             and video.shape[0] == 1
             and project_weight.shape[2] == 8 * HD
-            and video.shape[1] % (CHUNKS * TILE) == 0
+            and video.shape[1] % (sum(CHUNKS) * TILE) == 0
             and operands[7].shape[1] == 2 * video.shape[1] // TILE
             and video.shape[1] <= 256
         )

time: 72.6 us -> 71.2 us (0.981)
  Pallas kernels: 70.8 us -> 69.2 us
    pallas_call x1, Pallas kernels: 70.8 us -> 69.2 us  [layer_device(): pl.pallas_call(layer_kernel, out_shape=pltpu.VMEM((rows, 2 * columns), jn...]
where the time goes in v5:
time: 71.2 us; the launch traced here: 70 us
  Pallas kernels  69.2 us (97%)
  local copies, waits for them, and re-layouts  0.8 us (1%)
    pallas_call x1, Pallas kernels, layer_device(): pl.pallas_call(layer_kernel, out_shape=pltpu.VMEM((rows, 2 * columns), jn...  69.2 us

profile of v5, /device:TPU:3, one launch (start us, length us, event | category | flops | bytes accessed | tf_op | source)
XLA Modules:
  0.0 70.0 jit_solution(17067266786135144788)
XLA Ops:
  0.0 69.2 %shard_map.82 = bf16[128,2048]{1,0:T(8,128)(2,1)S(1)} custom-call(bf16[128,3072]{1,0:T(8,128)(2,1)} %bitcast.6, f32[1,3072]{1,0:T(1,128)} %shift_hbm.1, f32[1,3072]{1,0:T(1,128)} %scale_hbm.1, f32[3,1024]{1,0:T(4,128)} %bias_hbm.1, f32[1,128]{1,0:T(1,128)} %bitcast.8, f32[1,128]{1,0:T(1,128)} %bitcast.9, s32[12,1,16]{2,1,0:T(1,128)} %bitcast.7, ...), custom_call_target="tpu_custom_call" | custom-call | tf_op jit(solution)/shard_map/pallas_call | solution.py:662
  69.2 0.8 %copy.10 = bf16[1,128,2048]{2,1,0:T(8,128)(2,1)} copy(bf16[1,128,2048]{2,1,0:T(8,128)(2,1)S(1)} %bitcast.5) | data formatting | bytes 1048576

commit v6 on v5

--- a/solution.py
+++ b/solution.py
@@ -138,23 +138,26 @@
     def greet(target):
         pl.semaphore_signal(barrier, inc=1, device_id=target, device_id_type=MESH)
 
+    @pl.when(end)
+    def _():
+        for flip in range(2):
+            for k in range(4):
+                greet(at(k, flip, mate))
+
+    @pl.when(inner)
+    def _():
+        for flip in range(2):
+            for k in range(4):
+                greet(at(k, flip, far))
+        greet(at(0, 0, peer))
+
     for flip in range(2):
         for k in range(4):
             if k or flip:
                 greet(at(k, flip))
 
-    @pl.when(end)
-    def _():
-        for flip in range(2):
-            for k in range(4):
-                greet(at(k, flip, mate))
-
-    @pl.when(inner)
-    def _():
-        for flip in range(2):
-            for k in range(4):
-                greet(at(k, flip, far))
-        greet(at(0, 0, peer))
+    def half_video(group, place, side):
+        return (group * 8 + place // 2 * 4 + side * 2 + lax.rem(place, 2)) * rows
 
     def block(h, owner):
         return wbuf.at[h, pl.ds(pl.multiple_of(owner * slab, 16), slab), :]
@@ -189,7 +192,7 @@
             remote(
                 weight_ref.at[i, :, columns(pos(k), h)],
                 wbuf.at[h, mine, pl.ds(i * HD, HD)],
-                wsend.at[h, k - 1],
+                wsend,
                 wrecv.at[h, dp],
                 at(k),
             )
@@ -250,7 +253,7 @@
     sizes = [count * unit for count in CHUNKS]
 
     def norm_chunk(q):
-        half = pl.multiple_of((pos(0) * 2 + y) * rows + offsets[q], TILE)
+        half = pl.multiple_of(half_video(0, pos(0), y) + offsets[q], TILE)
 
         @pl.loop(0, sizes[q] // step)
         def _(n):
@@ -263,7 +266,7 @@
             tok[pl.ds(half + first, step), :] = normed.astype(jnp.bfloat16)
 
     def tokens_at(group, place, side, q):
-        first = (group * 8 + place * 2 + side) * rows + offsets[q]
+        first = half_video(group, place, side) + offsets[q]
         return tok.at[pl.ds(pl.multiple_of(first, TILE), sizes[q]), :]
 
     def token_send(group, place, side, q, target, to_group=None):
@@ -289,7 +292,7 @@
         token_send(group, place, side, q, at(1)).wait_recv()
 
     def wait_sibling_tokens(group, k, side):
-        first = (group * 8 + pos(k) * 2 + side) * rows
+        first = half_video(group, pos(k), side)
         extent = tok.at[pl.ds(pl.multiple_of(first, TILE), rows), :]
         remote(extent, extent, tsend, srecv.at[group, pos(k) // 2, side], at(1)).wait_recv()
 
@@ -389,8 +392,8 @@
             seen = lax.dot_general(rows_seen, in_tile, both, preferred_element_type=jnp.float32)
             masks[group * 4 + v] = jnp.where(seen > 0.5, 0.0, MASKED)
 
-    most = (jnp.where(z == 1, 0, 4 * slab), 12 * slab)
-    last = (far_peer * 4 * slab, 4 * slab)
+    most = (jnp.where(z == 1, 0, 2 * slab), 14 * slab)
+    last = (jnp.where(z == 1, 14 * slab, 0), 2 * slab)
     whole = (0, 16 * slab)
 
     def project(first, size, h, depth, add=False):
@@ -405,13 +408,16 @@
         project((group * 4 + pos(k) // 2 * 2) * total, 2 * total, h, depth, add)
 
     def project_sides(group, h, k, side, depth, add=False):
-        for m in range(2):
-            video = group * 4 + pos(k) // 2 * 2 + m
-            project((video * 2 + side) * rows, rows, h, depth, add)
+        project(half_video(group, pair(k), side), 2 * rows, h, depth, add)
 
     def attend(group, h, first, count):
-        block = pl.ds(pl.multiple_of((group * 4 + first) * total, TILE), count * total)
-        acc = accs[block, :]
+        acc = jnp.concatenate(
+            [
+                accs[pl.ds(pl.multiple_of(half_video(group, first + m, side), TILE), rows), :]
+                for m in range(count)
+                for side in range(2)
+            ]
+        )
         place = columns(pos(0), h)
         query = acc[:, 0:HD] + bias_ref[0:1, place]
         key = acc[:, HD : 2 * HD] + bias_ref[1:2, place]
@@ -476,9 +482,7 @@
         bytes_sent(tok, token_rows, tsend)
         bytes_sent(member, members, msend)
         bytes_sent(obuf, results * rows, osend)
-        for h in range(2):
-            for k in (1, 2, 3):
-                bytes_sent(wbuf.at[0], slab, wsend.at[h, k - 1])
+        bytes_sent(wbuf.at[0], 6 * slab, wsend)
 
     def outs_received(count):
         extent = out_ref.at[:, 0 : count * HD]
@@ -549,9 +553,16 @@
     for k in (2, 3, 1):
         start(piece_sends(1, k))
 
-    def relay_one(h, layer, k, role):
-        wait_block(h, layer * 4 + pos(k))
-        pass_on(h, layer, k, role)
+    def first_x(layer):
+        return 1 - layer // 3
+
+    def relay_place(layer, n):
+        early_x = first_x(layer)
+        owner = layer * 4 + (1 - early_x if n & 2 else early_x) * 2
+        owner = owner + (1 - core if n & 1 else core)
+        wait_block(1, owner)
+        for way, target in ways(1, layer, "inner"):
+            z_send(1, owner, way, target).start()
 
     def pass_tokens(group, which, q):
         place, copies = {
@@ -567,7 +578,16 @@
     @pl.when(end)
     def _():
         pass_direct()
-        own_layer(1, range(4), "end")
+        straight = x == first_x(z)
+
+        @pl.when(straight)
+        def _():
+            own_layer(1, (0, 1, 2, 3), "end")
+
+        @pl.when(jnp.logical_not(straight))
+        def _():
+            own_layer(1, (2, 3, 0, 1), "end")
+
         for q in (*chunks[1:], 0):
             pass_tokens(0, "diagonal", q)
             if q:
@@ -603,21 +623,23 @@
         attend_pair(0, 0, 0)
         for q in chunks:
             pass_tokens(0, "diagonal", q)
-        relay_one(1, far, 0, "inner")
+        relay_place(far, 0)
         for side in range(2):
             wait_sibling_tokens(0, 3, side)
         project_pair(0, 0, 2, whole)
         attend_pair(0, 0, 2, send=False)
-        relay_one(1, far, 1, "inner")
-        relay_one(1, far, 2, "inner")
+        relay_place(far, 1)
+        relay_place(far, 2)
         pass_tokens(1, "across", 0)
         send_pair(0, 0, 2)
-        relay_one(1, far, 3, "inner")
+        relay_place(far, 3)
         relay(1, [peer], "inner")
+        wait_members(1)
+        write_masks(1)
+        for n in range(2):
+            relay_place(far_peer, n)
         project_pair(0, 1, 0, most)
         project_pair(0, 1, 2, most)
-        wait_members(1)
-        write_masks(1)
         for q in chunks:
             pass_tokens(1, "beside", q)
         pass_tokens(1, "across", 1)
@@ -626,7 +648,8 @@
         wait_sibling_tokens(1, 3, y)
         project_sides(1, 1, 2, y, most)
         pass_tokens(1, "across", 2)
-        relay(1, [far_peer], "inner")
+        for n in range(2, 4):
+            relay_place(far_peer, n)
         project_pair(0, 1, 2, last, True)
         attend_pair(0, 1, 2)
         project_sides(1, 1, 0, y, last, True)
@@ -637,13 +660,16 @@
         for k in range(2):
             if k:
                 wait_sibling_tokens(1, 1, 1 - y)
-            project(((4 + pos(k)) * 2 + 1 - y) * rows, rows, 1, whole)
+            project(half_video(1, pos(k), 1 - y), rows, 1, whole)
             attend(1, 1, pos(k), 1)
             send_results(1, 1, pos(k), 1)
         project_sides(1, 1, 2, y, last, True)
-        wait_sibling_tokens(1, 3, 1 - y)
-        project_sides(1, 1, 2, 1 - y, whole)
-        attend_pair(1, 1, 2)
+        for k in range(2, 4):
+            if k == 3:
+                wait_sibling_tokens(1, 3, 1 - y)
+            project(half_video(1, pos(k), 1 - y), rows, 1, whole)
+            attend(1, 1, pos(k), 1)
+            send_results(1, 1, pos(k), 1)
         project_pair(0, 1, 0, last, True)
         attend_pair(0, 1, 0)
         outs_received(14)
@@ -674,7 +700,7 @@
             pltpu.VMEM((24 * rows, HD), jnp.bfloat16),
             dma((2,)),
             dma((7,)),
-            dma((2, 3)),
+            dma,
             dma((2,)),
             dma((2, 16)),
             dma,

time: 71.2 us -> 70.9 us (level)
  no operation moved by 1% of the time
where the time goes in v6:
time: 70.9 us; the launch traced here: 70 us
  Pallas kernels  69.2 us (98%)
  local copies, waits for them, and re-layouts  0.8 us (1%)
    pallas_call x1, Pallas kernels, layer_device(): pl.pallas_call(layer_kernel, out_shape=pltpu.VMEM((rows, 2 * columns), jn...  69.2 us

profile of v6, /device:TPU:3, one launch (start us, length us, event | category | flops | bytes accessed | tf_op | source)
XLA Modules:
  0.0 70.0 jit_solution(7659219386949765831)
XLA Ops:
  0.0 69.2 %shard_map.82 = bf16[128,2048]{1,0:T(8,128)(2,1)S(1)} custom-call(bf16[128,3072]{1,0:T(8,128)(2,1)} %bitcast.6, f32[1,3072]{1,0:T(1,128)} %shift_hbm.1, f32[1,3072]{1,0:T(1,128)} %scale_hbm.1, f32[3,1024]{1,0:T(4,128)} %bias_hbm.1, f32[1,128]{1,0:T(1,128)} %bitcast.8, f32[1,128]{1,0:T(1,128)} %bitcast.9, s32[12,1,16]{2,1,0:T(1,128)} %bitcast.7, ...), custom_call_target="tpu_custom_call" | custom-call | tf_op jit(solution)/shard_map/pallas_call | solution.py:688
  69.2 0.8 %copy.10 = bf16[1,128,2048]{2,1,0:T(8,128)(2,1)} copy(bf16[1,128,2048]{2,1,0:T(8,128)(2,1)S(1)} %bitcast.5) | data formatting | bytes 1048576

commit v7 on v6

--- a/solution.py
+++ b/solution.py
@@ -521,14 +521,14 @@
     def _():
         pl.semaphore_wait(barrier, 16)
 
-    for k in (2, 3, 1):
-        start(piece_sends(0, k))
-
     def first_sends(role):
-        start(member_sends(role))
+        own_layer(0, (0,), role)
+        for k in (2, 3, 1):
+            start(piece_sends(0, k))
         for q in range(early):
             start(own_tokens(q))
-        own_layer(0, (0, 1), role)
+        start(member_sends(role))
+        own_layer(0, (1,), role)
 
     @pl.when(end)
     def _():

time: 70.9 us -> 71 us (level)
  no operation moved by 1% of the time
where the time goes in v7:
time: 71 us; the launch traced here: 69.8 us
  Pallas kernels  69 us (97%)
  local copies, waits for them, and re-layouts  0.8 us (1%)
    pallas_call x1, Pallas kernels, layer_device(): pl.pallas_call(layer_kernel, out_shape=pltpu.VMEM((rows, 2 * columns), jn...  69 us

profile of v7, /device:TPU:3, one launch (start us, length us, event | category | flops | bytes accessed | tf_op | source)
XLA Modules:
  0.0 69.8 jit_solution(4203186778821866052)
XLA Ops:
  0.0 69.0 %shard_map.82 = bf16[128,2048]{1,0:T(8,128)(2,1)S(1)} custom-call(bf16[128,3072]{1,0:T(8,128)(2,1)} %bitcast.6, f32[1,3072]{1,0:T(1,128)} %shift_hbm.1, f32[1,3072]{1,0:T(1,128)} %scale_hbm.1, f32[3,1024]{1,0:T(4,128)} %bias_hbm.1, f32[1,128]{1,0:T(1,128)} %bitcast.8, f32[1,128]{1,0:T(1,128)} %bitcast.9, s32[12,1,16]{2,1,0:T(1,128)} %bitcast.7, ...), custom_call_target="tpu_custom_call" | custom-call | tf_op jit(solution)/shard_map/pallas_call | solution.py:688
  69.1 0.8 %copy.10 = bf16[1,128,2048]{2,1,0:T(8,128)(2,1)} copy(bf16[1,128,2048]{2,1,0:T(8,128)(2,1)S(1)} %bitcast.5) | data formatting | bytes 1048576
